TPU v7x, 512 devices: a whole 4x8x8 slice. The times are simulated.
512 devices in a mesh: rep: 64 (over z_hi, y, core), fsdp: 8 (over x, z_lo).
Axes of the slice: x: 4, y: 8, z: 8 (z_hi: 4, z_lo: 2; z = z_hi * 2 + z_lo), core: 2. Of those that a mesh axis runs over, the one named last changes fastest.
Arguments:
- anchor: float32 [4096, 512], P('fsdp', 'rep'), may hold values from -6 to 6
- momentum: float32 [4096, 512], P('fsdp', 'rep'), may hold values from -1.2 to 1.2
- tokens: bfloat16 [64, 2048, 4096], P('rep', 'fsdp'), may hold values from -6 to 6
- targets: bfloat16 [64, 2048, 512], P('rep', 'fsdp'), may hold values from -6 to 6
- first_moment: float32 [64, 4096, 512], P('rep', 'fsdp'), may hold values from -0.0018 to 0.0018
- second_moment: float32 [64, 4096, 512], P('rep', 'fsdp'), may hold values from 2e-08 to 2e-07
Outputs:
- anchor_next: float32 [4096, 512], P('fsdp', 'rep')
- momentum_next: float32 [4096, 512], P('fsdp', 'rep')
All inputs are finite; a program needn't handle non-finite values.
Results may differ from a plain program's by a relative error of at most 0.002.
Values may be sent and summed in bfloat16 or wider, within the bound.
No kernel may reach another device: no remote copies, remote signals or barrier semaphores. Data moves between devices by JAX's collectives and lax.ppermute only.
A program may use at most 64 MiB of HBM per device.

v0:
```python
import math
import jax
import jax.numpy as jnp
from jax import lax
from jax.sharding import PartitionSpec as P

beta_one = 0.9
beta_two = 0.95
adam_eps = 1e-08
inner_rate = 0.2
decay_rate = 0.1
outer_rate = 0.7
outer_mom = 0.9


def local(anchor, momentum, tokens, targets, first_moment, second_moment):
    own_columns = anchor.astype(jnp.bfloat16)
    start_rows = lax.all_gather(own_columns, "rep", axis=1, tiled=True)
    local_tokens = tokens[0]
    model_width = local_tokens.shape[1]
    groups = lax.axis_size("fsdp")
    count_tokens = local_tokens.shape[0] * groups
    columns = local_tokens
    projected = jnp.dot(
        columns,
        lax.all_gather(start_rows, "fsdp", axis=0, tiled=True),
        preferred_element_type=jnp.float32,
    )
    projected = projected * model_width ** (-0.5)
    residual = (projected - targets[0].astype(jnp.float32)).astype(jnp.bfloat16)
    columns = local_tokens
    summed = lax.psum_scatter(
        lax.dot_general(
            columns, residual, (((0,), (0,)), ((), ())), preferred_element_type=jnp.float32
        ).astype(jnp.bfloat16),
        "fsdp",
        scatter_dimension=0,
        tiled=True,
    ).astype(jnp.float32)
    gradient = summed * (1.0 / (math.sqrt(model_width) * count_tokens))
    moment_one = beta_one * first_moment[0] + (1.0 - beta_one) * gradient
    moment_two = beta_two * second_moment[0] + (1.0 - beta_two) * gradient * gradient
    direction = moment_one / (jnp.sqrt(moment_two) + adam_eps)
    update_delta = inner_rate * (direction + decay_rate * start_rows.astype(jnp.float32))
    owned_count = anchor.shape[1]
    total = lax.psum(update_delta, "rep")
    owned_sum = lax.dynamic_slice_in_dim(total, lax.axis_index("rep") * owned_count, owned_count, 1)
    mean_delta = owned_sum / lax.axis_size("rep")
    momentum_next = outer_mom * momentum + mean_delta
    anchor_next = anchor - outer_rate * (mean_delta + outer_mom * momentum_next)
    return (anchor_next, momentum_next)


def solution(mesh):
    placed = (
        P("fsdp", "rep"),
        P("fsdp", "rep"),
        P("rep", "fsdp", None),
        P("rep", "fsdp", None),
        P("rep", "fsdp", None),
        P("rep", "fsdp", None),
    )
    return jax.shard_map(
        local,
        mesh=mesh,
        in_specs=placed,
        out_specs=(P("fsdp", "rep"), P("fsdp", "rep")),
        check_vma=False,
    )
```

profile of v0, /device:TPU:1, one launch (start us, length us, event | category | flops | bytes accessed | tf_op | source)
XLA Modules:
  0.0 863.5 jit_solution(5334465605169246126)
XLA Ops:
  7.2 0.0 copy-start
  7.2 0.0 all-gather.2.cloned.1.call-start
  7.2 0.9 convert_element_type.24
  8.1 96.5 %all_gather.6 = bf16[512,512]{0,1:T(8,128)(2,1)} all-gather(bf16[512,8]{0,1:T(8,128)(2,1)S(1)} %convert_element_type.24), channel_id=1, replica_groups=mesh['rep'=64,'fsdp'=8] {'rep'}, dimensions={1}, use_global_device_ids=true | all-gather | bytes 532480 | tf_op jit(solution)/shard_map/all_gather | solution.py:18
  104.6 0.0 all-gather.2.cloned.1.call-update
  104.6 0.0 reduce-scatter.2.cloned.1.call-start
  104.6 87.4 %all-gather.2.cloned.1.call-done = bf16[4096,512]{0,1:T(8,128)(2,1)} async-done(((bf16[512,512]{0,1:T(8,128)(2,1)}), bf16[4096,512]{0,1:T(8,128)(2,1)}) %all-gather.2.cloned.1.call-update) | async-done | bytes 4194320 | tf_op jit(solution)/shard_map/all_gather | solution.py:26
  192.1 0.0 copy-done
  192.1 6.7 fusion
  198.8 0.0 copy-start.1
  198.8 0.0 reduce-scatter.2.cloned.1.call-update
  198.8 0.0 all-reduce.2.cloned.1.call-start
  198.9 2.6 copy.9
  201.5 0.0 copy-start.2
  201.5 0.0 copy-start.3
  201.5 2.5 copy.8
  204.0 91.6 %reduce-scatter.2.cloned.1.call-done = bf16[512,512]{0,1:T(8,128)(2,1)} async-done(((bf16[4096,512]{0,1:T(8,128)(2,1)}), bf16[512,512]{0,1:T(8,128)(2,1)}) %reduce-scatter.2.cloned.1.call-update) | async-done | bytes 524304 | tf_op jit(solution)/shard_map/reduce_scatter | solution.py:32
  295.6 0.0 copy-done.1
  295.6 3.5 fusion.18
  299.1 0.0 all-reduce.2.cloned.1.call-update
  299.1 556.5 %all-reduce.2.cloned.1.call-done = f32[512,512]{0,1:T(8,128)} async-done(((f32[512,512]{0,1:T(8,128)}), f32[512,512]{0,1:T(8,128)}) %all-reduce.2.cloned.1.call-update) | async-done | bytes 1048592 | tf_op jit(solution)/shard_map/psum | solution.py:46
  855.6 0.0 copy-done.2
  855.7 0.0 copy-done.3
  855.7 1.3 multiply_subtract_fusion
Async XLA Ops:
  7.2 184.9 %copy-start = (bf16[1,256,4096]{2,1,0:T(8,128)(2,1)S(1)}, bf16[1,256,4096]{2,1,0:T(8,128)(2,1)}, u32[]{:S(2)}) copy-start(bf16[1,256,4096]{2,1,0:T(8,128)(2,1)} %param.8) | copy-start | bytes 6291460
  7.2 184.9 %all-gather.2.cloned.1.call-start = ((), (), s32[]{:S(2)}) async-start(), calls=%async_computation.1 | async-start | bytes 4718592 | tf_op jit(solution)/shard_map/all_gather | solution.py:26
  104.6 191.0 %reduce-scatter.2.cloned.1.call-start = ((), (), s32[]{:S(2)}) async-start(), calls=%async_computation.2 | async-start | bytes 4718592 | tf_op jit(solution)/shard_map/reduce_scatter | solution.py:32
  198.8 96.8 %copy-start.1 = (bf16[512,512]{0,1:T(8,128)(2,1)S(1)}, bf16[512,512]{0,1:T(8,128)(2,1)}, u32[]{:S(2)}) copy-start(bf16[512,512]{0,1:T(8,128)(2,1)} %all_gather.6) | copy-start | bytes 1572868
  198.8 656.8 %all-reduce.2.cloned.1.call-start = ((), (), s32[]{:S(2)}) async-start(), calls=%async_computation.3 | async-start | bytes 2097152 | tf_op jit(solution)/shard_map/psum | solution.py:46
  201.5 654.2 %copy-start.2 = (f32[512,8]{0,1:T(8,128)S(1)}, f32[512,8]{0,1:T(8,128)}, u32[]{:S(2)}) copy-start(f32[512,8]{0,1:T(8,128)} %param.6) | copy-start | bytes 49156
  201.5 654.2 %copy-start.3 = (f32[512,8]{0,1:T(8,128)S(1)}, f32[512,8]{0,1:T(8,128)}, u32[]{:S(2)}) copy-start(f32[512,8]{0,1:T(8,128)} %param.7) | copy-start | bytes 49156
Sparse Core Ops, SparseCore 0:
  104.7 87.3 all-gather.1
  198.9 96.6 reduce-scatter.1
  299.3 556.3 all-reduce.1
where the time goes:
time: 864 us
  waiting for transfers between devices  736 us (85%)
  blocking collectives  96.5 us (11%)
  between operations  13.8 us (2%)
    psum x1, waiting for transfers between devices, local(): total = lax.psum(update_delta, 'rep')  557 us
    all_gather x1, blocking collectives, local(): start_rows = lax.all_gather(own_columns, 'rep', axis=1, tiled=True)  96.5 us
    reduce_scatter x1, waiting for transfers between devices, local(): lax.psum_scatter(lax.dot_general(columns, residual, (((0,), (0,)), ((), (...  91.6 us
    all_gather x1, waiting for transfers between devices, local(): lax.all_gather(start_rows, 'fsdp', axis=0, tiled=True)  87.4 us
  transfers between devices with their start and end apart: 3, of which 3 were waited for; matrix products, arithmetic and copies ran while one was open for 1% of the time, Pallas kernels for 0%

commit v1 on v0

--- a/solution.py
+++ b/solution.py
@@ -23,7 +23,9 @@
     columns = local_tokens
     projected = jnp.dot(
         columns,
-        lax.all_gather(start_rows, "fsdp", axis=0, tiled=True),
+        jnp.concatenate(
+            lax.all_to_all(jnp.stack([start_rows] * lax.axis_size("fsdp")), "fsdp", 0, 0), axis=0
+        ),
         preferred_element_type=jnp.float32,
     )
     projected = projected * model_width ** (-0.5)

time: 864 us -> 816 us (0.944)
  waiting for transfers between devices: 736 us -> 638 us
  blocking collectives: 96.5 us -> 145 us
    all_gather x1 -> x0, waiting for transfers between devices: 87.4 us -> none  [local(): lax.all_gather(start_rows, 'fsdp', axis=0, tiled=True)]
    all_to_all x0 -> x1, blocking collectives: none -> 54 us  [local(): lax.all_to_all(jnp.stack([start_rows] * lax.axis_size('fsdp')), 'fsdp', 0...]
    reduce_scatter x1, waiting for transfers between devices: 91.6 us -> 81.5 us  [local(): lax.psum_scatter(lax.dot_general(columns, residual, (((0,), (0,)), ((), (...]
  transfers between devices with their start and end apart: 3 -> 2, of which waited for: 3 -> 2; matrix products, arithmetic and copies ran while one was open for 1% -> 1% of each run, Pallas kernels for 0% -> 0%
where the time goes in v1:
time: 816 us
  waiting for transfers between devices  638 us (78%)
  blocking collectives  145 us (18%)
  between operations  14.1 us (2%)
    psum x1, waiting for transfers between devices, local(): total = lax.psum(update_delta, 'rep')  557 us
    all_gather x1, blocking collectives, local(): start_rows = lax.all_gather(own_columns, 'rep', axis=1, tiled=True)  91.3 us
    reduce_scatter x1, waiting for transfers between devices, local(): lax.psum_scatter(lax.dot_general(columns, residual, (((0,), (0,)), ((), (...  81.5 us
    all_to_all x1, blocking collectives, local(): lax.all_to_all(jnp.stack([start_rows] * lax.axis_size('fsdp')), 'fsdp', 0...  54 us
  transfers between devices with their start and end apart: 2, of which 2 were waited for; matrix products, arithmetic and copies ran while one was open for 1% of the time, Pallas kernels for 0%

profile of v1, /device:TPU:1, one launch (start us, length us, event | category | flops | bytes accessed | tf_op | source)
XLA Modules:
  0.0 815.8 jit_solution(17300351686176064336)
XLA Ops:
  7.2 0.0 copy-start
  7.2 0.0 reduce-scatter.2.cloned.1.call-start
  7.2 0.9 convert_element_type.24
  8.1 91.3 %all_gather.3 = bf16[512,512]{0,1:T(8,128)(2,1)S(1)} all-gather(bf16[512,8]{0,1:T(8,128)(2,1)S(1)} %convert_element_type.24), channel_id=1, replica_groups=mesh['rep'=64,'fsdp'=8] {'rep'}, dimensions={1}, use_global_device_ids=true | all-gather | bytes 532480 | tf_op jit(solution)/shard_map/all_gather | solution.py:18
  99.4 0.2 copy.9
  99.6 0.4 stack.2
  99.9 0.0 copy-start.1
  100.0 54.0 %all_to_all.5 = bf16[8,512,512]{2,1,0:T(8,128)(2,1)} all-to-all(bf16[8,512,512]{2,1,0:T(8,128)(2,1)S(1)} %stack.2), channel_id=1, replica_groups=mesh['rep'=64,'fsdp'=8] {'fsdp'}, dimensions={0} | all-to-all | bytes 8388608 | tf_op jit(solution)/shard_map/all_to_all | solution.py:27
  154.0 0.0 copy-done
  154.0 0.0 copy-done.1
  154.0 6.6 fusion
  160.6 0.0 reduce-scatter.2.cloned.1.call-update
  160.7 0.0 all-reduce.2.cloned.1.call-start
  160.7 2.6 copy.10
  163.3 0.0 copy-start.2
  163.3 0.0 copy-start.3
  163.3 2.6 copy.8
  165.8 81.5 %reduce-scatter.2.cloned.1.call-done = bf16[512,512]{0,1:T(8,128)(2,1)} async-done(((bf16[4096,512]{0,1:T(8,128)(2,1)}), bf16[512,512]{0,1:T(8,128)(2,1)}) %reduce-scatter.2.cloned.1.call-update) | async-done | bytes 524304 | tf_op jit(solution)/shard_map/reduce_scatter | solution.py:34
  247.3 3.5 fusion.18
  250.8 0.0 all-reduce.2.cloned.1.call-update
  250.8 556.8 %all-reduce.2.cloned.1.call-done = f32[512,512]{0,1:T(8,128)} async-done(((f32[512,512]{0,1:T(8,128)}), f32[512,512]{0,1:T(8,128)}) %all-reduce.2.cloned.1.call-update) | async-done | bytes 1048592 | tf_op jit(solution)/shard_map/psum | solution.py:48
  807.6 0.0 copy-done.2
  807.6 0.0 copy-done.3
  807.6 1.3 multiply_subtract_fusion
Async XLA Ops:
  7.2 146.8 %copy-start = (bf16[1,256,4096]{2,1,0:T(8,128)(2,1)S(1)}, bf16[1,256,4096]{2,1,0:T(8,128)(2,1)}, u32[]{:S(2)}) copy-start(bf16[1,256,4096]{2,1,0:T(8,128)(2,1)} %param.8) | copy-start | bytes 6291460
  7.2 240.1 %reduce-scatter.2.cloned.1.call-start = ((), (), s32[]{:S(2)}) async-start(), calls=%async_computation.2 | async-start | bytes 4718592 | tf_op jit(solution)/shard_map/reduce_scatter | solution.py:34
  99.9 54.0 %copy-start.1 = (bf16[1,256,512]{2,1,0:T(8,128)(2,1)S(1)}, bf16[1,256,512]{2,1,0:T(8,128)(2,1)}, u32[]{:S(2)}) copy-start(bf16[1,256,512]{2,1,0:T(8,128)(2,1)} %param.9) | copy-start | bytes 786436
  160.7 646.9 %all-reduce.2.cloned.1.call-start = ((), (), s32[]{:S(2)}) async-start(), calls=%async_computation.3 | async-start | bytes 2097152 | tf_op jit(solution)/shard_map/psum | solution.py:48
  163.3 644.3 %copy-start.2 = (f32[512,8]{0,1:T(8,128)S(1)}, f32[512,8]{0,1:T(8,128)}, u32[]{:S(2)}) copy-start(f32[512,8]{0,1:T(8,128)} %param.6) | copy-start | bytes 49156
  163.3 644.3 %copy-start.3 = (f32[512,8]{0,1:T(8,128)S(1)}, f32[512,8]{0,1:T(8,128)}, u32[]{:S(2)}) copy-start(f32[512,8]{0,1:T(8,128)} %param.7) | copy-start | bytes 49156
Sparse Core Ops, SparseCore 0:
  160.8 86.4 reduce-scatter.1
  250.9 556.5 all-reduce.1
